TPU v7x, 512 devices: a whole 4x8x8 slice. The times are simulated.
512 devices in a mesh: chan: 32 (over y, x), row: 16 (over z, core).
Axes of the slice: x: 4, y: 8, z: 8, core: 2. Of those that a mesh axis runs over, the one named last changes fastest.
Arguments:
- amplitudes: bfloat16 [32, 3072, 2048], P('chan', 'row'), may hold values from -6 to 6
- interaction: bfloat16 [32, 2048, 2048], P('chan', 'row'), as said below
- weights6j: float32 [32, 2048], P('chan'), may hold values from -1.5 to 1.5
- column_order: int32 [32, 2048], P('chan'), may hold values from 0 to 2047, each once within a row
- row_counts: int32 [32], P('chan'), may hold values from 768 to 3072, as said below
Outputs:
- pp_update: bfloat16 [32, 3072, 2048], P('chan', 'row')
Inputs may be any that keep to these rules, and one draw needn't show every extreme that they name: Each channel's interaction block is symmetric. `row_counts`: some channel has all 3072 rows live and some channel exactly 768 in every draw.
All inputs are finite; a program needn't handle non-finite values.
Results may differ from a plain program's by a relative error of at most 0.005.
Values may be sent and summed in bfloat16 or wider, within the bound.
No kernel may reach another device: no remote copies, remote signals or barrier semaphores. Data moves between devices by JAX's collectives and lax.ppermute only.
A program may use at most 64 MiB of HBM per device.

v0:
```python
import jax
import jax.numpy as jnp
from jax import lax
from jax.sharding import PartitionSpec as P


def per_device(amplitudes, interaction, weights6j, column_order, row_counts):
    own_block = amplitudes[0]
    row_count = own_block.shape[0]
    col_count = own_block.shape[1]
    v_panel = interaction[0]
    col_order = column_order[0]
    col_weight = weights6j[0]
    gathered = lax.all_to_all(own_block, "chan", split_axis=1, concat_axis=1, tiled=True)
    row_start = lax.axis_index("row") * row_count
    live_rows = row_start + jnp.arange(row_count, dtype=jnp.int32) < row_counts[0]
    taken = jnp.take(gathered, col_order, axis=1).astype(jnp.float32) * col_weight[None, :]
    recoupled = jnp.where(live_rows[:, None], taken, jnp.float32(0.0)).astype(jnp.bfloat16)
    product = jnp.dot(
        recoupled,
        lax.all_gather(v_panel, "row", axis=0, tiled=True),
        preferred_element_type=jnp.float32,
    )
    scaled = (product * col_weight[None, :]).astype(jnp.bfloat16)
    inverse = (
        jnp.zeros((col_count,), jnp.int32).at[col_order].set(jnp.arange(col_count, dtype=jnp.int32))
    )
    restored = jnp.take(scaled, inverse, axis=1)
    returned = lax.all_to_all(restored, "chan", split_axis=1, concat_axis=1, tiled=True)
    return returned[None]


def solution(mesh):
    in_specs = (
        P("chan", "row", None),
        P("chan", "row", None),
        P("chan", None),
        P("chan", None),
        P("chan"),
    )
    out_specs = P("chan", "row", None)
    return jax.shard_map(
        per_device, mesh=mesh, in_specs=in_specs, out_specs=out_specs, check_vma=False
    )
```

profile of v0, /device:TPU:2, one launch (start us, length us, event | category | flops | bytes accessed | tf_op | source)
XLA Modules:
  0.0 133.4 jit_solution(3425176206983938947)
XLA Ops:
  6.5 0.0 all-gather.3.cloned.1.call-start
  6.5 0.7 all-gather.3.cloned.1.call-update
  7.3 0.0 copy-start
  7.3 2.3 %copy.10 = bf16[1,192,2048]{1,2,0:T(8,128)(2,1)} copy(bf16[1,192,2048]{2,1,0:T(8,128)(2,1)} %param.7) | data formatting | bytes 1572864 | tf_op args[0]
  9.5 10.2 %all-to-all-start = ((bf16[192,32,64]{0,2,1:T(8,128)(2,1)}), bf16[192,32,64]{0,2,1:T(8,128)(2,1)S(1)}, u32[]{:S(2)}, u32[]{:S(2)}) async-start(bf16[192,32,64]{0,2,1:T(8,128)(2,1)} %bitcast.4), calls=%async_computation | async-start | bytes 2097152 | tf_op jit(solution)/shard_map/all_to_all | solution.py:14
  20.4 0.0 copy-done
  20.5 8.0 %scatter_custom_fusion = s32[2048]{0:T(1024)S(1)} fusion(s32[2048]{0:T(1024)S(1)} %bitcast.30, s32[2048]{0:T(1024)S(1)} %iota.9, s32[]{:T(128)} %constant.4.clone.1), kind=kCustom, calls=%fused_computation.23 | custom fusion | bytes 8196 | tf_op jit(solution)/shard_map/scatter | solution.py:26
  28.6 19.2 %all-to-all-done = bf16[192,32,64]{0,2,1:T(8,128)(2,1)S(1)} async-done(((bf16[192,32,64]{0,2,1:T(8,128)(2,1)}), bf16[192,32,64]{0,2,1:T(8,128)(2,1)S(1)}, u32[]{:S(2)}, u32[]{:S(2)}) %all-to-all-start) | async-done | bytes 786464 | tf_op jit(solution)/shard_map/all_to_all | solution.py:14
  47.8 7.5 %gather_fusion = bf16[2048,192]{1,0:T(8,128)(2,1)S(1)} fusion(bf16[192,2048]{0,1:T(8,128)(2,1)S(1)} %bitcast.25, s32[2048]{0:T(1024)S(1)} %fusion.15), kind=kCustom, calls=%fused_computation.clone | custom fusion | bytes 1581056 | tf_op jit(solution)/shard_map/jit(_take)/gather | solution.py:17
  55.3 0.0 copy-start.1
  55.4 0.5 copy.11
  55.9 17.6 %all-gather.3.cloned.1.call-done = bf16[1,2048,2048]{2,1,0:T(8,128)(2,1)} async-done(((bf16[1,128,2048]{2,1,0:T(8,128)(2,1)}), bf16[1,2048,2048]{2,1,0:T(8,128)(2,1)}) %all-gather.3.cloned.1.call-update) | async-done | bytes 8388624 | tf_op jit(solution)/shard_map/all_gather | solution.py:21
  73.5 0.0 copy-done.1
  73.5 5.2 %fusion.5 = bf16[192,2048]{1,0:T(8,128)(2,1)S(1)} fusion(bf16[1,2048,2048]{2,1,0:T(8,128)(2,1)} %all-gather.3.cloned.1.call-done, bf16[2048,192]{0,1:T(8,128)(2,1)S(1)} %copy.11, f32[2048]{0:T(1024)S(1)} %bitcast.31, pred[192]{0:T(512)(128)(4,1)S(1)} %add_compare_fusion, pred[2048]{0:T(1024)(128)(4,1)S(1)} %compare_and_fusion.1), kind=kOutput, calls=%fused_computation.6 | convolution fusion | flops 1613365248 | bytes 9971904 | tf_op jit(solution)/shard_map/dot_general | solution.py:19
  78.7 0.5 copy.12
  79.3 7.5 %gather_fusion.1 = bf16[2048,192]{1,0:T(8,128)(2,1)S(1)} fusion(bf16[192,2048]{0,1:T(8,128)(2,1)S(1)} %copy.12, s32[2048]{0:T(1024)S(1)} %fusion.16), kind=kCustom, calls=%fused_computation.1.clone | custom fusion | bytes 1581056 | tf_op jit(solution)/shard_map/jit(_take)/gather | solution.py:28
  86.8 0.4 broadcast_select_fusion
  87.2 38.1 %all_to_all.21 = bf16[192,32,64]{0,2,1:T(8,128)(2,1)S(1)} all-to-all(bf16[192,32,64]{0,2,1:T(8,128)(2,1)S(1)} %bitcast.26), channel_id=1, replica_groups=mesh['chan'=32,'row'=16] {'chan'}, dimensions={1} | all-to-all | bytes 1572864 | tf_op jit(solution)/shard_map/all_to_all | solution.py:29
  125.4 1.2 copy.13
  (7 shorter events, 0.1 us)
Async XLA Ops:
  6.5 67.0 %all-gather.3.cloned.1.call-start = ((), (), s32[]{:S(2)}) async-start(), calls=%async_computation.2 | async-start | bytes 8912896 | tf_op jit(solution)/shard_map/all_gather | solution.py:21
  7.3 13.2 %copy-start = (s32[1,2048]{1,0:T(1,128)S(1)}, s32[1,2048]{1,0:T(1,128)}, u32[]{:S(2)}) copy-start(s32[1,2048]{1,0:T(1,128)} %param.10) | copy-start | bytes 24580
  9.5 38.3 %all-to-all-start = ((bf16[192,32,64]{0,2,1:T(8,128)(2,1)}), bf16[192,32,64]{0,2,1:T(8,128)(2,1)S(1)}, u32[]{:S(2)}, u32[]{:S(2)}) async-start(bf16[192,32,64]{0,2,1:T(8,128)(2,1)} %bitcast.4), calls=%async_computation | async-start | bytes 2097152 | tf_op jit(solution)/shard_map/all_to_all | solution.py:14
  55.3 18.1 %copy-start.1 = (f32[1,2048]{1,0:T(1,128)S(1)}, f32[1,2048]{1,0:T(1,128)}, u32[]{:S(2)}) copy-start(f32[1,2048]{1,0:T(1,128)} %param.9) | copy-start | bytes 24580
Sparse Core Ops, SparseCore 0:
  9.5 63.9 all-gather.2
where the time goes:
time: 134 us; the launch traced here: 133 us
  blocking collectives  38.1 us (28%)
  waiting for transfers between devices  37.6 us (28%)
  local copies, waits for them, and re-layouts  27.6 us (21%)
  between operations  14.2 us (11%)
  starting transfers between devices  10.2 us (8%)
  matrix products  5.23 us (4%)
    all_to_all x1, blocking collectives, per_device(): lax.all_to_all(restored, 'chan', split_axis=1, concat_axis=1, tiled=True)  38.1 us
    all_to_all x1, waiting for transfers between devices, per_device(): lax.all_to_all(own_block, 'chan', split_axis=1, concat_axis=1, tiled=True)  19.2 us
    all_gather x1, waiting for transfers between devices, per_device(): lax.all_gather(v_panel, 'row', axis=0, tiled=True)  17.6 us
    all_to_all x1, starting transfers between devices, per_device(): lax.all_to_all(own_block, 'chan', split_axis=1, concat_axis=1, tiled=True)  10.2 us
    scatter x1, local copies, waits for them, and re-layouts, per_device(): jnp.zeros((col_count,), jnp.int32).at[col_order]  8.05 us
    gather x2, local copies, waits for them, and re-layouts, per_device(): jnp.take(gathered, col_order, axis=1).astype(jnp.float32)  7.99 us
    gather x1, local copies, waits for them, and re-layouts, per_device(): restored = jnp.take(scaled, inverse, axis=1)  7.5 us
    dot_general x1, matrix products, per_device(): jnp.dot(recoupled, lax.all_gather(v_panel, 'row', axis=0, tiled=True), pr...  5.23 us
  transfers between devices with their start and end apart: 2, of which 2 were waited for; matrix products, arithmetic and copies ran while one was open for 14% of the time, Pallas kernels for 0%

commit v1 on v0

--- a/solution.py
+++ b/solution.py
@@ -2,6 +2,11 @@
 import jax.numpy as jnp
 from jax import lax
 from jax.sharding import PartitionSpec as P
+
+
+def swapped_in(block, axis, dim):
+    sent = jnp.stack([block] * lax.axis_size(axis))
+    return jnp.concatenate(lax.all_to_all(sent, axis, 0, 0), axis=dim)
 
 
 def per_device(amplitudes, interaction, weights6j, column_order, row_counts):
@@ -16,11 +21,7 @@
     live_rows = row_start + jnp.arange(row_count, dtype=jnp.int32) < row_counts[0]
     taken = jnp.take(gathered, col_order, axis=1).astype(jnp.float32) * col_weight[None, :]
     recoupled = jnp.where(live_rows[:, None], taken, jnp.float32(0.0)).astype(jnp.bfloat16)
-    product = jnp.dot(
-        recoupled,
-        lax.all_gather(v_panel, "row", axis=0, tiled=True),
-        preferred_element_type=jnp.float32,
-    )
+    product = jnp.dot(recoupled, swapped_in(v_panel, "row", 0), preferred_element_type=jnp.float32)
     scaled = (product * col_weight[None, :]).astype(jnp.bfloat16)
     inverse = (
         jnp.zeros((col_count,), jnp.int32).at[col_order].set(jnp.arange(col_count, dtype=jnp.int32))

time: 134 us -> 287 us (2.14)
  waiting for transfers between devices: 37.6 us -> 167 us
  blocking collectives: 38.1 us -> 71.3 us
  between operations: 14.2 us -> 0.79 us
  local copies, waits for them, and re-layouts: 27.6 us -> 31.1 us
    all_to_all x1, waiting for transfers between devices: 19.2 us -> 167 us  [swapped_in(): return jnp.concatenate(lax.all_to_all(sent, axis, 0, 0), axis=dim)]
    all_to_all x0 -> x1, blocking collectives: none -> 38.1 us  [per_device(): lax.all_to_all(own_block, 'chan', split_axis=1, concat_axis=1, tiled=True)]
    all_gather x1 -> x0, waiting for transfers between devices: 17.6 us -> none  [per_device(): lax.all_gather(v_panel, 'row', axis=0, tiled=True)]
    all_to_all x1, blocking collectives: 38.1 us -> 33.2 us  [per_device(): lax.all_to_all(restored, 'chan', split_axis=1, concat_axis=1, tiled=True)]
    another operation x0 -> x1, local copies, waits for them, and re-layouts: none -> 4.32 us  [swapped_in(): sent = jnp.stack([block] * lax.axis_size(axis))]
  transfers between devices with their start and end apart: 2 -> 1, of which waited for: 2 -> 1; matrix products, arithmetic and copies ran while one was open for 14% -> 6% of each run, Pallas kernels for 0% -> 0%
where the time goes in v1:
time: 287 us
  waiting for transfers between devices  167 us (58%)
  blocking collectives  71.3 us (25%)
  local copies, waits for them, and re-layouts  31.1 us (11%)
  starting transfers between devices  10.6 us (4%)
  matrix products  5.24 us (2%)
    all_to_all x1, waiting for transfers between devices, swapped_in(): return jnp.concatenate(lax.all_to_all(sent, axis, 0, 0), axis=dim)  167 us
    all_to_all x1, blocking collectives, per_device(): lax.all_to_all(own_block, 'chan', split_axis=1, concat_axis=1, tiled=True)  38.1 us
    all_to_all x1, blocking collectives, per_device(): lax.all_to_all(restored, 'chan', split_axis=1, concat_axis=1, tiled=True)  33.2 us
    all_to_all x1, starting transfers between devices, swapped_in(): return jnp.concatenate(lax.all_to_all(sent, axis, 0, 0), axis=dim)  10.6 us
    scatter x1, local copies, waits for them, and re-layouts, per_device(): jnp.zeros((col_count,), jnp.int32).at[col_order]  8.05 us
    gather x2, local copies, waits for them, and re-layouts, per_device(): jnp.take(gathered, col_order, axis=1).astype(jnp.float32)  8 us
    gather x1, local copies, waits for them, and re-layouts, per_device(): restored = jnp.take(scaled, inverse, axis=1)  7.5 us
  transfers between devices with their start and end apart: 1, of which 1 were waited for; matrix products, arithmetic and copies ran while one was open for 6% of the time, Pallas kernels for 0%

profile of v1, /device:TPU:2, one launch (start us, length us, event | category | flops | bytes accessed | tf_op | source)
XLA Modules:
  0.0 287.0 jit_solution(4492723865463700360)
XLA Ops:
  0.0 0.0 copy-start
  0.0 1.5 copy.10
  1.5 38.1 %all_to_all.26 = bf16[192,32,64]{0,2,1:T(8,128)(2,1)S(1)} all-to-all(bf16[192,32,64]{0,2,1:T(8,128)(2,1)S(1)} %bitcast.24), channel_id=1, replica_groups=mesh['chan'=32,'row'=16] {'chan'}, dimensions={1} | all-to-all | bytes 1572864 | tf_op jit(solution)/shard_map/all_to_all | solution.py:19
  39.6 0.0 copy-done
  39.6 4.3 %stack.3 = bf16[16,128,2048]{2,1,0:T(8,128)(2,1)} broadcast(bf16[128,2048]{1,0:T(8,128)(2,1)S(1)} %bitcast.25), dimensions={1,2} | broadcast | bytes 8912896 | tf_op jit(solution)/shard_map/stack | solution.py:8
  43.9 0.0 copy-start.1
  43.9 10.6 %all-to-all-start.1 = ((bf16[16,128,2048]{2,1,0:T(8,128)(2,1)}), bf16[16,128,2048]{2,1,0:T(8,128)(2,1)}, u32[]{:S(2)}, u32[]{:S(2)}) async-start(bf16[16,128,2048]{2,1,0:T(8,128)(2,1)} %stack.3), calls=%async_computation.1 | async-start | bytes 16777216 | tf_op jit(solution)/shard_map/all_to_all | solution.py:9
  55.2 0.0 copy-done.1
  55.2 8.0 %scatter_custom_fusion = s32[2048]{0:T(1024)S(1)} fusion(s32[2048]{0:T(1024)S(1)} %bitcast.28, s32[2048]{0:T(1024)S(1)} %iota.9, s32[]{:T(128)} %constant.4.clone.1), kind=kCustom, calls=%fused_computation.21 | custom fusion | bytes 8196 | tf_op jit(solution)/shard_map/scatter | solution.py:27
  63.4 7.5 %gather_fusion = bf16[2048,192]{1,0:T(8,128)(2,1)S(1)} fusion(bf16[192,2048]{0,1:T(8,128)(2,1)S(1)} %bitcast.21, s32[2048]{0:T(1024)S(1)} %fusion.8), kind=kCustom, calls=%fused_computation.clone | custom fusion | bytes 1581056 | tf_op jit(solution)/shard_map/jit(_take)/gather | solution.py:22
  70.9 0.0 copy-start.2
  70.9 0.5 copy.11
  71.4 167.4 %all-to-all-done.1 = bf16[16,128,2048]{2,1,0:T(8,128)(2,1)} async-done(((bf16[16,128,2048]{2,1,0:T(8,128)(2,1)}), bf16[16,128,2048]{2,1,0:T(8,128)(2,1)}, u32[]{:S(2)}, u32[]{:S(2)}) %all-to-all-start.1) | async-done | bytes 8388640 | tf_op jit(solution)/shard_map/all_to_all | solution.py:9
  238.8 0.0 copy-done.2
  238.8 5.2 %fusion = bf16[192,2048]{1,0:T(8,128)(2,1)S(1)} fusion(bf16[2048,2048]{1,0:T(8,128)(2,1)} %bitcast.9, bf16[2048,192]{0,1:T(8,128)(2,1)S(1)} %copy.11, f32[2048]{0:T(1024)S(1)} %bitcast.29, pred[192]{0:T(512)(128)(4,1)S(1)} %add_compare_fusion, pred[2048]{0:T(1024)(128)(4,1)S(1)} %compare_and_fusion.1), kind=kOutput, calls=%fused_computation.4 | convolution fusion | flops 1613365248 | bytes 9971904 | tf_op jit(solution)/shard_map/dot_general | solution.py:24
  244.0 0.5 copy.12
  244.6 7.5 %gather_fusion.1 = bf16[2048,192]{1,0:T(8,128)(2,1)S(1)} fusion(bf16[192,2048]{0,1:T(8,128)(2,1)S(1)} %copy.12, s32[2048]{0:T(1024)S(1)} %fusion.9), kind=kCustom, calls=%fused_computation.1.clone | custom fusion | bytes 1581056 | tf_op jit(solution)/shard_map/jit(_take)/gather | solution.py:29
  252.1 0.4 broadcast_select_fusion
  252.5 33.2 %all_to_all.27 = bf16[192,32,64]{0,2,1:T(8,128)(2,1)S(1)} all-to-all(bf16[192,32,64]{0,2,1:T(8,128)(2,1)S(1)} %bitcast.22), channel_id=1, replica_groups=mesh['chan'=32,'row'=16] {'chan'}, dimensions={1} | all-to-all | bytes 1572864 | tf_op jit(solution)/shard_map/all_to_all | solution.py:30
  285.8 1.2 copy.13
  (7 shorter events, 0.1 us)
Async XLA Ops:
  0.0 39.6 %copy-start = (bf16[1,128,2048]{2,1,0:T(8,128)(2,1)S(1)}, bf16[1,128,2048]{2,1,0:T(8,128)(2,1)}, u32[]{:S(2)}) copy-start(bf16[1,128,2048]{2,1,0:T(8,128)(2,1)} %param.8) | copy-start | bytes 1572868
  43.9 11.3 %copy-start.1 = (s32[1,2048]{1,0:T(1,128)S(1)}, s32[1,2048]{1,0:T(1,128)}, u32[]{:S(2)}) copy-start(s32[1,2048]{1,0:T(1,128)} %param.10) | copy-start | bytes 24580
  43.9 194.9 %all-to-all-start.1 = ((bf16[16,128,2048]{2,1,0:T(8,128)(2,1)}), bf16[16,128,2048]{2,1,0:T(8,128)(2,1)}, u32[]{:S(2)}, u32[]{:S(2)}) async-start(bf16[16,128,2048]{2,1,0:T(8,128)(2,1)} %stack.3), calls=%async_computation.1 | async-start | bytes 16777216 | tf_op jit(solution)/shard_map/all_to_all | solution.py:9
  70.9 167.9 %copy-start.2 = (f32[1,2048]{1,0:T(1,128)S(1)}, f32[1,2048]{1,0:T(1,128)}, u32[]{:S(2)}) copy-start(f32[1,2048]{1,0:T(1,128)} %param.9) | copy-start | bytes 24580
